TPU v7x, 32 devices: a whole 2x2x4 slice. The times are simulated.
32 devices in a mesh: wide: 8 (over z, x), grp: 4 (over y, core).
Axes of the slice: x: 2, y: 2, z: 4, core: 2. Of those that a mesh axis runs over, the one named last changes fastest.
Arguments:
- query_rows: bfloat16 [4096, 1280], P(('wide', 'grp')), may hold values from -9 to 9, as said below
- key_rows: bfloat16 [4096, 1280], P(('wide', 'grp')), may hold values from -9 to 9, as said below
- value_rows: bfloat16 [4096, 1280], P(('wide', 'grp')), may hold values from -6 to 6
- block_image: int32 [32], replicated, may hold values from 0 to 6, never falling along the last dimension, each value on 1 to 8 neighbouring positions
Outputs:
- attended: bfloat16 [4096, 1280], P(('wide', 'grp'))
Inputs may be any that keep to these rules, and one draw needn't show every extreme that they name: `query_rows`: Queries: entries bounded as stated. `key_rows`: Keys: entries bounded as stated. `block_image`: image numbers never fall along the window; every image covers 1 to 8 whole blocks and one covers exactly 8.
All inputs are finite; a program needn't handle non-finite values.
Results may differ from a plain program's by a relative error of at most 0.004.
Values may be sent and summed in bfloat16 or wider, within the bound.
A program may use at most 64 MiB of HBM per device.

v0:
```python
import math
import jax
import jax.numpy as jnp
from jax import lax
from jax.sharding import PartitionSpec as P

HDIM = 80
BLK = 128
MOST = 8
neg_large = -1e30


def from_behind(value, axis, steps):
    count = lax.axis_size(axis)
    leading, last = (max(0, -steps), min(count, count - steps))
    return lax.ppermute(value, axis, [(source, source + steps) for source in range(leading, last)])


def block_tokens(block_ids, block_rows):
    return jnp.broadcast_to(block_ids[:, None], (block_ids.shape[0], block_rows)).reshape(-1)


def fold_tile(totals, query_ids, query_head, key_head, value_head, key_ids, scale_value):
    live_pairs = query_ids[:, None] == key_ids[None, :]
    acc_out, run_max, run_den = totals
    scores = (
        jnp.einsum("qhd,khd->qhk", query_head, key_head, preferred_element_type=jnp.float32)
        * scale_value
    )
    scores = jnp.where(live_pairs[:, None, :], scores, neg_large)
    new_max = jnp.maximum(run_max, jnp.max(scores, axis=-1))
    weights = jnp.where(live_pairs[:, None, :], jnp.exp(scores - new_max[..., None]), 0.0)
    fading = jnp.exp(run_max - new_max)
    run_den = run_den * fading + jnp.sum(weights, axis=-1)
    acc_out = acc_out * fading[..., None] + jnp.einsum(
        "qhk,khd->qhd", weights.astype(jnp.bfloat16), value_head, preferred_element_type=jnp.float32
    )
    return (acc_out, new_max, run_den)


def fold_keys(totals, query_ids, query_head, key_head, value_head, key_ids, scale_value):
    current = tuple((member for member in totals))
    current = fold_tile(current, query_ids, query_head, key_head, value_head, key_ids, scale_value)
    return current


def body(query_rows, key_rows, value_rows, block_image):
    stacked = jnp.stack((query_rows, key_rows, value_rows))
    regrouped = lax.all_to_all(stacked, "grp", split_axis=2, concat_axis=1, tiled=True)
    local_rows = regrouped.shape[1]
    head_count = regrouped.shape[2] // HDIM
    shaped = regrouped.reshape(3, local_rows, head_count, HDIM)
    query_head = shaped[0]
    key_value = shaped[1:]
    blocks_here = local_rows // BLK
    wide_count = lax.axis_size("wide")
    position = lax.axis_index("wide")
    scale_value = 1.0 / math.sqrt(HDIM)
    query_ids = block_tokens(
        lax.dynamic_slice_in_dim(block_image, position * blocks_here, blocks_here), BLK
    )

    def source_ids(source):
        inside = (source >= 0) & (source < wide_count)
        clipped = jnp.clip(source, 0, wide_count - 1)
        found_ids = block_tokens(
            lax.dynamic_slice_in_dim(block_image, clipped * blocks_here, blocks_here), BLK
        )
        return jnp.where(inside, found_ids, -2)

    totals = (
        jnp.zeros((local_rows, head_count, HDIM), jnp.float32),
        jnp.full((local_rows, head_count), neg_large, jnp.float32),
        jnp.zeros((local_rows, head_count), jnp.float32),
    )
    reach_steps = min(wide_count - 1, (MOST + blocks_here - 2) // blocks_here)
    totals = fold_keys(
        totals, query_ids, query_head, key_value[0], key_value[1], query_ids, scale_value
    )
    for distance in range(1, reach_steps + 1):
        arrived = from_behind(key_value, "wide", distance)
        totals = fold_keys(
            totals,
            query_ids,
            query_head,
            arrived[0],
            arrived[1],
            source_ids(position - distance),
            scale_value,
        )
        arrived = from_behind(key_value, "wide", -distance)
        totals = fold_keys(
            totals,
            query_ids,
            query_head,
            arrived[0],
            arrived[1],
            source_ids(position + distance),
            scale_value,
        )
    acc_out, run_max, run_den = totals
    result = (
        (acc_out / run_den[..., None]).astype(jnp.bfloat16).reshape(local_rows, head_count * HDIM)
    )
    restored = lax.all_to_all(result, "grp", split_axis=0, concat_axis=1, tiled=True)
    return restored


def solution(mesh):
    return jax.shard_map(
        body,
        mesh=mesh,
        in_specs=(
            P(("wide", "grp"), None),
            P(("wide", "grp"), None),
            P(("wide", "grp"), None),
            P(),
        ),
        out_specs=P(("wide", "grp"), None),
        check_vma=False,
    )
```

profile of v0, /device:TPU:24, one launch (start us, length us, event | category | flops | bytes accessed | tf_op | source)
XLA Modules:
  0.0 93.7 jit_solution(12908256977121639371)
XLA Ops:
  0.0 1.3 %pad_maximum_fusion = bf16[3,128,1280]{2,1,0:T(8,128)(2,1)S(1)} fusion(bf16[1,128,1280]{2,1,0:T(8,128)(2,1)} %bitcast.190, bf16[1,128,1280]{2,1,0:T(8,128)(2,1)} %bitcast.191, bf16[1,128,1280]{2,1,0:T(8,128)(2,1)} %bitcast.192), kind=kLoop, calls=%fused_computation.51 | loop fusion | flops 983040 | bytes 1966080 | tf_op jit(solution)/shard_map/stack | solution.py:48
  1.3 2.2 %copy.41 = bf16[3,128,1280]{1,0,2:T(4,128)(2,1)} copy(bf16[3,128,1280]{2,1,0:T(8,128)(2,1)S(1)} %pad_maximum_fusion) | data formatting | bytes 1966080 | tf_op jit(solution)/shard_map/stack | solution.py:48
  3.5 3.5 %all-to-all-start = ((bf16[3,128,1280]{1,0,2:T(4,128)(2,1)}), bf16[3,128,1280]{1,0,2:T(4,128)(2,1)S(1)}, u32[]{:S(2)}, u32[]{:S(2)}) async-start(bf16[3,128,1280]{1,0,2:T(4,128)(2,1)} %copy.41), calls=%async_computation | async-start | bytes 2621440 | tf_op jit(solution)/shard_map/all_to_all | solution.py:49
  7.4 16.9 %all-to-all-done = bf16[3,128,1280]{1,0,2:T(4,128)(2,1)S(1)} async-done(((bf16[3,128,1280]{1,0,2:T(4,128)(2,1)}), bf16[3,128,1280]{1,0,2:T(4,128)(2,1)S(1)}, u32[]{:S(2)}, u32[]{:S(2)}) %all-to-all-start) | async-done | bytes 983072 | tf_op jit(solution)/shard_map/all_to_all | solution.py:49
  24.9 1.1 %slice.48 = bf16[2,512,4,80]{1,3,2,0:T(8,128)(2,1)} reshape(bf16[2,4,128,320]{2,1,3,0:T(4,128)(2,1)S(1)} %copy.47) | data formatting | bytes 1310720 | tf_op jit(solution)/shard_map/slice | solution.py:54
  26.0 3.3 %collective-permute-start.1 = (bf16[2,512,4,80]{1,3,2,0:T(8,128)(2,1)}, bf16[2,512,4,80]{1,3,2,0:T(8,128)(2,1)}, u32[]{:S(2)}, u32[]{:S(2)}) collective-permute-start(bf16[2,512,4,80]{1,3,2,0:T(8,128)(2,1)} %slice.48), channel_id=1, source_target_pairs={{4,0},{8,4},{12,8},{16,12},{20,16},{24,20},{28,24},{5,1},{9,5},{13... | collective-permute-start | bytes 1966088 | tf_op jit(solution)/shard_map/ppermute | solution.py:16
  30.2 3.2 %collective-permute-start.3 = (bf16[2,512,4,80]{1,3,2,0:T(8,128)(2,1)}, bf16[2,512,4,80]{1,3,2,0:T(8,128)(2,1)}, u32[]{:S(2)}, u32[]{:S(2)}) collective-permute-start(bf16[2,512,4,80]{1,3,2,0:T(8,128)(2,1)} %slice.48), channel_id=1, source_target_pairs={{8,0},{12,4},{16,8},{20,12},{24,16},{28,20},{9,1},{13,5},{17,9},{2... | collective-permute-start | bytes 1966088 | tf_op jit(solution)/shard_map/ppermute | solution.py:16
  33.4 1.3 %collective-permute-start.2 = (bf16[2,512,4,80]{1,3,2,0:T(8,128)(2,1)}, bf16[2,512,4,80]{1,3,2,0:T(8,128)(2,1)}, u32[]{:S(2)}, u32[]{:S(2)}) collective-permute-start(bf16[2,512,4,80]{1,3,2,0:T(8,128)(2,1)} %slice.48), channel_id=1, source_target_pairs={{0,8},{4,12},{8,16},{12,20},{16,24},{20,28},{1,9},{5,13},{9,17},{1... | collective-permute-start | bytes 1966088 | tf_op jit(solution)/shard_map/ppermute | solution.py:16
  34.7 2.7 %collective-permute-start = (bf16[2,512,4,80]{1,3,2,0:T(8,128)(2,1)}, bf16[2,512,4,80]{1,3,2,0:T(8,128)(2,1)}, u32[]{:S(2)}, u32[]{:S(2)}) collective-permute-start(bf16[2,512,4,80]{1,3,2,0:T(8,128)(2,1)} %slice.48), channel_id=1, source_target_pairs={{0,4},{4,8},{8,12},{12,16},{16,20},{20,24},{24,28},{1,5},{5,9},{9,... | collective-permute-start | bytes 1966088 | tf_op jit(solution)/shard_map/ppermute | solution.py:16
  39.7 5.1 %collective-permute-done.1 = bf16[2,512,4,80]{1,3,2,0:T(8,128)(2,1)} collective-permute-done((bf16[2,512,4,80]{1,3,2,0:T(8,128)(2,1)}, bf16[2,512,4,80]{1,3,2,0:T(8,128)(2,1)}, u32[]{:S(2)}, u32[]{:S(2)}) %collective-permute-start.1) | collective-permute-done | bytes 655392 | tf_op jit(solution)/shard_map/ppermute | solution.py:16
  44.8 1.9 %fusion.2 = (f32[512,4]{0,1:T(4,128)S(1)}, f32[4,512,512]{2,1,0:T(8,128)S(1)}) fusion(pred[512,512]{0,1:T(8,128)(4,1)S(1)} %get-tuple-element.20, bf16[512,4,80]{0,2,1:T(8,128)(2,1)S(1)} %squeeze.34, bf16[2,512,4,80]{1,3,2,0:T(8,128)(2,1)} %collective-permute-done.1), kind=kOutput, calls=%fused_computation.12 | convolution fusion | flops 170915840 | bytes 5120000 | tf_op jit(solution)/shard_map/qhd,khd->qhk/dot_general | solution.py:27
  46.7 4.5 %collective-permute-done.2 = bf16[2,512,4,80]{1,3,2,0:T(8,128)(2,1)} collective-permute-done((bf16[2,512,4,80]{1,3,2,0:T(8,128)(2,1)}, bf16[2,512,4,80]{1,3,2,0:T(8,128)(2,1)}, u32[]{:S(2)}, u32[]{:S(2)}) %collective-permute-start.2) | collective-permute-done | bytes 655392 | tf_op jit(solution)/shard_map/ppermute | solution.py:16
  51.2 1.9 %fusion.3 = (f32[512,4]{0,1:T(4,128)S(1)}, f32[4,512,512]{2,1,0:T(8,128)S(1)}) fusion(pred[512,512]{0,1:T(8,128)(4,1)S(1)} %get-tuple-element.21, bf16[512,4,80]{0,2,1:T(8,128)(2,1)S(1)} %squeeze.34, bf16[2,512,4,80]{1,3,2,0:T(8,128)(2,1)} %collective-permute-done.2), kind=kOutput, calls=%fused_computation.13 | convolution fusion | flops 170915840 | bytes 5120000 | tf_op jit(solution)/shard_map/qhd,khd->qhk/dot_general | solution.py:27
  53.2 4.2 %collective-permute-done.3 = bf16[2,512,4,80]{1,3,2,0:T(8,128)(2,1)} collective-permute-done((bf16[2,512,4,80]{1,3,2,0:T(8,128)(2,1)}, bf16[2,512,4,80]{1,3,2,0:T(8,128)(2,1)}, u32[]{:S(2)}, u32[]{:S(2)}) %collective-permute-start.3) | collective-permute-done | bytes 655392 | tf_op jit(solution)/shard_map/ppermute | solution.py:16
  57.4 1.9 %fusion.4 = (f32[512,4]{0,1:T(4,128)S(1)}, f32[4,512,512]{2,1,0:T(8,128)S(1)}) fusion(pred[512,512]{0,1:T(8,128)(4,1)S(1)} %get-tuple-element.22, bf16[512,4,80]{0,2,1:T(8,128)(2,1)S(1)} %squeeze.34, bf16[2,512,4,80]{1,3,2,0:T(8,128)(2,1)} %collective-permute-done.3), kind=kOutput, calls=%fused_computation.14 | convolution fusion | flops 170915840 | bytes 5120000 | tf_op jit(solution)/shard_map/qhd,khd->qhk/dot_general | solution.py:27
  59.4 6.0 %collective-permute-done = bf16[2,512,4,80]{1,3,2,0:T(8,128)(2,1)} collective-permute-done((bf16[2,512,4,80]{1,3,2,0:T(8,128)(2,1)}, bf16[2,512,4,80]{1,3,2,0:T(8,128)(2,1)}, u32[]{:S(2)}, u32[]{:S(2)}) %collective-permute-start) | collective-permute-done | bytes 655392 | tf_op jit(solution)/shard_map/ppermute | solution.py:16
  65.4 1.9 %fusion.1 = (f32[512,4]{0,1:T(4,128)S(1)}, f32[4,512,512]{2,1,0:T(8,128)S(1)}) fusion(pred[512,512]{0,1:T(8,128)(4,1)S(1)} %get-tuple-element.23, bf16[512,4,80]{0,2,1:T(8,128)(2,1)S(1)} %squeeze.34, bf16[2,512,4,80]{1,3,2,0:T(8,128)(2,1)} %collective-permute-done), kind=kOutput, calls=%fused_computation.11 | convolution fusion | flops 170915840 | bytes 5120000 | tf_op jit(solution)/shard_map/qhd,khd->qhk/dot_general | solution.py:27
  70.5 1.1 %fusion.5 = f32[512,4]{0,1:T(4,128)S(1)} fusion(f32[4,512,512]{2,1,0:T(8,128)S(1)} %get-tuple-element.38, f32[512,4]{0,1:T(4,128)S(1)} %get-tuple-element.18, pred[512,512]{0,1:T(8,128)(4,1)S(1)} %get-tuple-element.19), kind=kLoop, calls=%fused_computation.15 | loop fusion | flops 5240832 | bytes 4472832 | tf_op jit(solution)/shard_map/reduce_sum | solution.py:34
  72.7 1.5 %fusion.69 = f32[512,4,80]{0,2,1:T(8,128)S(1)} fusion(bf16[512,4,80]{0,2,1:T(8,128)(2,1)S(1)} %squeeze.35, f32[4,512,512]{2,1,0:T(8,128)S(1)} %get-tuple-element.38, f32[512,4]{0,1:T(4,128)S(1)} %get-tuple-element.18, pred[512,512]{0,1:T(8,128)(4,1)S(1)} %get-tuple-element.19, f32[512,4]{0,1:T(4,128)S(1)} %get-tuple-element.9, ...), kind=kOutput, calls=%fused_computation.48 | convolution fusion | flops 173342720 | bytes 5464064 | tf_op jit(solution)/shard_map/qhk,khd->qhd/dot_general | solution.py:35
  74.2 2.3 %fusion.42 = f32[512,4,80]{0,2,1:T(8,128)S(1)} fusion(f32[4,512,512]{2,1,0:T(8,128)S(1)} %get-tuple-element.30, f32[512,4]{0,1:T(4,128)S(1)} %get-tuple-element.10, pred[512,512]{0,1:T(8,128)(4,1)S(1)} %get-tuple-element.22, bf16[2,512,4,80]{1,3,2,0:T(8,128)(2,1)} %collective-permute-done.3), kind=kOutput, calls=%fused_computation.39 | convolution fusion | flops 173015040 | bytes 5447680 | tf_op jit(solution)/shard_map/qhk,khd->qhd/dot_general | solution.py:35
  76.5 2.3 %fusion.39 = f32[512,4,80]{0,2,1:T(8,128)S(1)} fusion(f32[4,512,512]{2,1,0:T(8,128)S(1)} %get-tuple-element.32, f32[512,4]{0,1:T(4,128)S(1)} %get-tuple-element.11, pred[512,512]{0,1:T(8,128)(4,1)S(1)} %get-tuple-element.21, bf16[2,512,4,80]{1,3,2,0:T(8,128)(2,1)} %collective-permute-done.2), kind=kOutput, calls=%fused_computation.38 | convolution fusion | flops 173015040 | bytes 5447680 | tf_op jit(solution)/shard_map/qhk,khd->qhd/dot_general | solution.py:35
  78.8 2.3 %fusion.36 = f32[512,4,80]{0,2,1:T(8,128)S(1)} fusion(f32[4,512,512]{2,1,0:T(8,128)S(1)} %get-tuple-element.34, f32[512,4]{0,1:T(4,128)S(1)} %get-tuple-element.12, pred[512,512]{0,1:T(8,128)(4,1)S(1)} %get-tuple-element.20, bf16[2,512,4,80]{1,3,2,0:T(8,128)(2,1)} %collective-permute-done.1), kind=kOutput, calls=%fused_computation.37 | convolution fusion | flops 173015040 | bytes 5447680 | tf_op jit(solution)/shard_map/qhk,khd->qhd/dot_general | solution.py:35
  81.1 2.4 %fusion.75 = bf16[512,4,80]{0,2,1:T(8,128)(2,1)S(1)} fusion(f32[512,4,80]{0,2,1:T(8,128)S(1)} %fusion.42, f32[512,4,80]{0,2,1:T(8,128)S(1)} %fusion.39, f32[512,4,80]{0,2,1:T(8,128)S(1)} %fusion.36, f32[512,4,80]{0,2,1:T(8,128)S(1)} %fusion.69, f32[4,512,512]{2,1,0:T(8,128)S(1)} %get-tuple-element.36, f32[512,4]{0,1:T(4,128)S(1)} %get-tuple-element.13, ...), kind=kOutput, calls=%fused_computation.50 | convolution fusion | flops 174489600 | bytes 7774208 | tf_op jit(solution)/shard_map/qhk,khd->qhd/dot_general | solution.py:35
  83.7 9.1 %all_to_all.34 = bf16[4,128,320]{1,2,0:T(8,128)(2,1)S(1)} all-to-all(bf16[4,128,320]{1,2,0:T(8,128)(2,1)S(1)} %copy.52), channel_id=1, replica_groups=mesh['wide'=8,'grp'=4] {'grp'}, dimensions={0} | all-to-all | bytes 655360 | tf_op jit(solution)/shard_map/all_to_all | solution.py:105
  (27 shorter events, 9.3 us)
Async XLA Ops:
  0.0 7.0 %copy-start = (s32[32]{0:T(128)S(1)}, s32[32]{0:T(128)}, u32[]{:S(2)}) copy-start(s32[32]{0:T(128)} %param.7) | copy-start | bytes 388
  3.5 20.8 %all-to-all-start = ((bf16[3,128,1280]{1,0,2:T(4,128)(2,1)}), bf16[3,128,1280]{1,0,2:T(4,128)(2,1)S(1)}, u32[]{:S(2)}, u32[]{:S(2)}) async-start(bf16[3,128,1280]{1,0,2:T(4,128)(2,1)} %copy.41), calls=%async_computation | async-start | bytes 2621440 | tf_op jit(solution)/shard_map/all_to_all | solution.py:49
  26.0 18.7 %collective-permute-start.1 = (bf16[2,512,4,80]{1,3,2,0:T(8,128)(2,1)}, bf16[2,512,4,80]{1,3,2,0:T(8,128)(2,1)}, u32[]{:S(2)}, u32[]{:S(2)}) collective-permute-start(bf16[2,512,4,80]{1,3,2,0:T(8,128)(2,1)} %slice.48), channel_id=1, source_target_pairs={{4,0},{8,4},{12,8},{16,12},{20,16},{24,20},{28,24},{5,1},{9,5},{13... | collective-permute-start | bytes 1966088 | tf_op jit(solution)/shard_map/ppermute | solution.py:16
  30.2 27.2 %collective-permute-start.3 = (bf16[2,512,4,80]{1,3,2,0:T(8,128)(2,1)}, bf16[2,512,4,80]{1,3,2,0:T(8,128)(2,1)}, u32[]{:S(2)}, u32[]{:S(2)}) collective-permute-start(bf16[2,512,4,80]{1,3,2,0:T(8,128)(2,1)} %slice.48), channel_id=1, source_target_pairs={{8,0},{12,4},{16,8},{20,12},{24,16},{28,20},{9,1},{13,5},{17,9},{2... | collective-permute-start | bytes 1966088 | tf_op jit(solution)/shard_map/ppermute | solution.py:16
  33.4 17.8 %collective-permute-start.2 = (bf16[2,512,4,80]{1,3,2,0:T(8,128)(2,1)}, bf16[2,512,4,80]{1,3,2,0:T(8,128)(2,1)}, u32[]{:S(2)}, u32[]{:S(2)}) collective-permute-start(bf16[2,512,4,80]{1,3,2,0:T(8,128)(2,1)} %slice.48), channel_id=1, source_target_pairs={{0,8},{4,12},{8,16},{12,20},{16,24},{20,28},{1,9},{5,13},{9,17},{1... | collective-permute-start | bytes 1966088 | tf_op jit(solution)/shard_map/ppermute | solution.py:16
  34.7 30.7 %collective-permute-start = (bf16[2,512,4,80]{1,3,2,0:T(8,128)(2,1)}, bf16[2,512,4,80]{1,3,2,0:T(8,128)(2,1)}, u32[]{:S(2)}, u32[]{:S(2)}) collective-permute-start(bf16[2,512,4,80]{1,3,2,0:T(8,128)(2,1)} %slice.48), channel_id=1, source_target_pairs={{0,4},{4,8},{8,12},{12,16},{16,20},{20,24},{24,28},{1,5},{5,9},{9,... | collective-permute-start | bytes 1966088 | tf_op jit(solution)/shard_map/ppermute | solution.py:16
where the time goes:
time: 94.3 us; the launch traced here: 93.7 us
  waiting for transfers between devices  36.7 us (39%)
  matrix products  19.6 us (21%)
  starting transfers between devices  14 us (15%)
  blocking collectives  9.08 us (10%)
  other arithmetic  7.57 us (8%)
  local copies, waits for them, and re-layouts  6.44 us (7%)
    ppermute x4, waiting for transfers between devices, from_behind(): lax.ppermute(value, axis, [(source, source + steps) for source in range(l...  19.9 us
    all_to_all x1, waiting for transfers between devices, body(): lax.all_to_all(stacked, 'grp', split_axis=2, concat_axis=1, tiled=True)  16.9 us
    dot_general x5, matrix products, fold_tile(): jnp.einsum('qhk,khd->qhd', weights.astype(jnp.bfloat16), value_head, pref...  10.9 us
    ppermute x4, starting transfers between devices, from_behind(): lax.ppermute(value, axis, [(source, source + steps) for source in range(l...  10.5 us
    all_to_all x1, blocking collectives, body(): lax.all_to_all(result, 'grp', split_axis=0, concat_axis=1, tiled=True)  9.08 us
    dot_general x5, matrix products, fold_tile(): jnp.einsum('qhd,khd->qhk', query_head, key_head, preferred_element_type=j...  8.72 us
    reduce_sum x5, other arithmetic, fold_tile(): run_den = run_den * fading + jnp.sum(weights, axis=-1)  5.27 us
    all_to_all x1, starting transfers between devices, body(): lax.all_to_all(stacked, 'grp', split_axis=2, concat_axis=1, tiled=True)  3.54 us
  transfers between devices with their start and end apart: 5, of which 5 were waited for; matrix products, arithmetic and copies ran while one was open for 10% of the time, Pallas kernels for 0%

commit v1 on v0

--- a/solution.py
+++ b/solution.py
@@ -46,7 +46,10 @@
 
 def body(query_rows, key_rows, value_rows, block_image):
     stacked = jnp.stack((query_rows, key_rows, value_rows))
-    regrouped = lax.all_to_all(stacked, "grp", split_axis=2, concat_axis=1, tiled=True)
+    regrouped = jnp.concatenate(
+        lax.all_to_all(jnp.stack(jnp.split(stacked, lax.axis_size("grp"), axis=2)), "grp", 0, 0),
+        axis=1,
+    )
     local_rows = regrouped.shape[1]
     head_count = regrouped.shape[2] // HDIM
     shaped = regrouped.reshape(3, local_rows, head_count, HDIM)

time: 94.3 us -> 92 us (0.976)
  waiting for transfers between devices: 36.7 us -> 33.2 us
  local copies, waits for them, and re-layouts: 6.44 us -> 7.74 us
    unnamed x2 -> x5, local copies, waits for them, and re-layouts: 0.01 us -> 3.56 us
    all_to_all x1, waiting for transfers between devices: 16.9 us -> 13.4 us  [body(): lax.all_to_all(jnp.stack(jnp.split(stacked, lax.axis_size('grp'), axis=2)...]
    another operation x1, local copies, waits for them, and re-layouts: 2.18 us -> 0.07 us  [body(): jnp.stack(jnp.split(stacked, lax.axis_size('grp'), axis=2))]
    another operation x1, other arithmetic: 1.29 us -> 0.11 us  [body(): stacked = jnp.stack((query_rows, key_rows, value_rows))]
    another operation x0 -> x1, other arithmetic: none -> 1.08 us  [body(): jnp.stack(jnp.split(stacked, lax.axis_size('grp'), axis=2))]
where the time goes in v1:
time: 92 us; the launch traced here: 91.3 us
  waiting for transfers between devices  33.2 us (36%)
  matrix products  19.6 us (21%)
  starting transfers between devices  14 us (15%)
  blocking collectives  9.08 us (10%)
  local copies, waits for them, and re-layouts  7.74 us (8%)
  other arithmetic  7.47 us (8%)
    ppermute x4, waiting for transfers between devices, from_behind(): lax.ppermute(value, axis, [(source, source + steps) for source in range(l...  19.9 us
    all_to_all x1, waiting for transfers between devices, body(): lax.all_to_all(jnp.stack(jnp.split(stacked, lax.axis_size('grp'), axis=2)...  13.4 us
    dot_general x5, matrix products, fold_tile(): jnp.einsum('qhk,khd->qhd', weights.astype(jnp.bfloat16), value_head, pref...  10.9 us
    ppermute x4, starting transfers between devices, from_behind(): lax.ppermute(value, axis, [(source, source + steps) for source in range(l...  10.5 us
    all_to_all x1, blocking collectives, body(): lax.all_to_all(result, 'grp', split_axis=0, concat_axis=1, tiled=True)  9.08 us
    dot_general x5, matrix products, fold_tile(): jnp.einsum('qhd,khd->qhk', query_head, key_head, preferred_element_type=j...  8.73 us
    reduce_sum x5, other arithmetic, fold_tile(): run_den = run_den * fading + jnp.sum(weights, axis=-1)  5.27 us
    unnamed x5, local copies, waits for them, and re-layouts  3.56 us
  transfers between devices with their start and end apart: 5, of which 5 were waited for; matrix products, arithmetic and copies ran while one was open for 10% of the time, Pallas kernels for 0%

profile of v1, /device:TPU:24, one launch (start us, length us, event | category | flops | bytes accessed | tf_op | source)
XLA Modules:
  0.0 91.3 jit_solution(7949446375103990647)
XLA Ops:
  0.0 1.2 %copy.26 = bf16[128,1280]{0,1:T(8,128)(2,1)S(1)} copy(bf16[128,1280]{1,0:T(8,128)(2,1)} %param.4) | data formatting | bytes 655360 | tf_op args[0]
  1.2 1.2 %copy.27 = bf16[128,1280]{0,1:T(8,128)(2,1)S(1)} copy(bf16[128,1280]{1,0:T(8,128)(2,1)} %param.5) | data formatting | bytes 655360 | tf_op args[1]
  2.4 1.2 %copy.28 = bf16[128,1280]{0,1:T(8,128)(2,1)S(1)} copy(bf16[128,1280]{1,0:T(8,128)(2,1)} %param.6) | data formatting | bytes 655360 | tf_op args[2]
  4.8 3.5 %all-to-all-start = ((bf16[4,3,128,320]{2,3,1,0:T(8,128)(2,1)}), bf16[4,3,128,320]{2,3,1,0:T(8,128)(2,1)S(1)}, u32[]{:S(2)}, u32[]{:S(2)}) async-start(bf16[4,3,128,320]{2,3,1,0:T(8,128)(2,1)} %pad_maximum_fusion.1), calls=%async_computation | async-start | bytes 1966080 | tf_op jit(solution)/shard_map/all_to_all | solution.py:50
  8.7 13.4 %all-to-all-done = bf16[4,3,128,320]{2,3,1,0:T(8,128)(2,1)S(1)} async-done(((bf16[4,3,128,320]{2,3,1,0:T(8,128)(2,1)}), bf16[4,3,128,320]{2,3,1,0:T(8,128)(2,1)S(1)}, u32[]{:S(2)}, u32[]{:S(2)}) %all-to-all-start) | async-done | bytes 983072 | tf_op jit(solution)/shard_map/all_to_all | solution.py:50
  22.6 1.1 %slice.48 = bf16[2,512,4,80]{1,3,2,0:T(8,128)(2,1)} reshape(bf16[2,4,128,320]{2,1,3,0:T(4,128)(2,1)S(1)} %copy.33) | data formatting | bytes 1310720 | tf_op jit(solution)/shard_map/slice | solution.py:57
  23.7 3.3 %collective-permute-start.1 = (bf16[2,512,4,80]{1,3,2,0:T(8,128)(2,1)}, bf16[2,512,4,80]{1,3,2,0:T(8,128)(2,1)}, u32[]{:S(2)}, u32[]{:S(2)}) collective-permute-start(bf16[2,512,4,80]{1,3,2,0:T(8,128)(2,1)} %slice.48), channel_id=1, source_target_pairs={{4,0},{8,4},{12,8},{16,12},{20,16},{24,20},{28,24},{5,1},{9,5},{13... | collective-permute-start | bytes 1966088 | tf_op jit(solution)/shard_map/ppermute | solution.py:16
  27.9 3.2 %collective-permute-start.3 = (bf16[2,512,4,80]{1,3,2,0:T(8,128)(2,1)}, bf16[2,512,4,80]{1,3,2,0:T(8,128)(2,1)}, u32[]{:S(2)}, u32[]{:S(2)}) collective-permute-start(bf16[2,512,4,80]{1,3,2,0:T(8,128)(2,1)} %slice.48), channel_id=1, source_target_pairs={{8,0},{12,4},{16,8},{20,12},{24,16},{28,20},{9,1},{13,5},{17,9},{2... | collective-permute-start | bytes 1966088 | tf_op jit(solution)/shard_map/ppermute | solution.py:16
  31.1 1.3 %collective-permute-start.2 = (bf16[2,512,4,80]{1,3,2,0:T(8,128)(2,1)}, bf16[2,512,4,80]{1,3,2,0:T(8,128)(2,1)}, u32[]{:S(2)}, u32[]{:S(2)}) collective-permute-start(bf16[2,512,4,80]{1,3,2,0:T(8,128)(2,1)} %slice.48), channel_id=1, source_target_pairs={{0,8},{4,12},{8,16},{12,20},{16,24},{20,28},{1,9},{5,13},{9,17},{1... | collective-permute-start | bytes 1966088 | tf_op jit(solution)/shard_map/ppermute | solution.py:16
  32.4 2.7 %collective-permute-start = (bf16[2,512,4,80]{1,3,2,0:T(8,128)(2,1)}, bf16[2,512,4,80]{1,3,2,0:T(8,128)(2,1)}, u32[]{:S(2)}, u32[]{:S(2)}) collective-permute-start(bf16[2,512,4,80]{1,3,2,0:T(8,128)(2,1)} %slice.48), channel_id=1, source_target_pairs={{0,4},{4,8},{8,12},{12,16},{16,20},{20,24},{24,28},{1,5},{5,9},{9,... | collective-permute-start | bytes 1966088 | tf_op jit(solution)/shard_map/ppermute | solution.py:16
  37.4 5.1 %collective-permute-done.1 = bf16[2,512,4,80]{1,3,2,0:T(8,128)(2,1)} collective-permute-done((bf16[2,512,4,80]{1,3,2,0:T(8,128)(2,1)}, bf16[2,512,4,80]{1,3,2,0:T(8,128)(2,1)}, u32[]{:S(2)}, u32[]{:S(2)}) %collective-permute-start.1) | collective-permute-done | bytes 655392 | tf_op jit(solution)/shard_map/ppermute | solution.py:16
  42.5 1.9 %fusion.2 = (f32[512,4]{0,1:T(4,128)S(1)}, f32[4,512,512]{2,1,0:T(8,128)S(1)}) fusion(pred[512,512]{0,1:T(8,128)(4,1)S(1)} %get-tuple-element.24, bf16[512,4,80]{0,2,1:T(8,128)(2,1)S(1)} %squeeze.34, bf16[2,512,4,80]{1,3,2,0:T(8,128)(2,1)} %collective-permute-done.1), kind=kOutput, calls=%fused_computation.12 | convolution fusion | flops 170915840 | bytes 5120000 | tf_op jit(solution)/shard_map/qhd,khd->qhk/dot_general | solution.py:27
  44.4 4.5 %collective-permute-done.2 = bf16[2,512,4,80]{1,3,2,0:T(8,128)(2,1)} collective-permute-done((bf16[2,512,4,80]{1,3,2,0:T(8,128)(2,1)}, bf16[2,512,4,80]{1,3,2,0:T(8,128)(2,1)}, u32[]{:S(2)}, u32[]{:S(2)}) %collective-permute-start.2) | collective-permute-done | bytes 655392 | tf_op jit(solution)/shard_map/ppermute | solution.py:16
  48.9 1.9 %fusion.3 = (f32[512,4]{0,1:T(4,128)S(1)}, f32[4,512,512]{2,1,0:T(8,128)S(1)}) fusion(pred[512,512]{0,1:T(8,128)(4,1)S(1)} %get-tuple-element.25, bf16[512,4,80]{0,2,1:T(8,128)(2,1)S(1)} %squeeze.34, bf16[2,512,4,80]{1,3,2,0:T(8,128)(2,1)} %collective-permute-done.2), kind=kOutput, calls=%fused_computation.13 | convolution fusion | flops 170915840 | bytes 5120000 | tf_op jit(solution)/shard_map/qhd,khd->qhk/dot_general | solution.py:27
  50.9 4.2 %collective-permute-done.3 = bf16[2,512,4,80]{1,3,2,0:T(8,128)(2,1)} collective-permute-done((bf16[2,512,4,80]{1,3,2,0:T(8,128)(2,1)}, bf16[2,512,4,80]{1,3,2,0:T(8,128)(2,1)}, u32[]{:S(2)}, u32[]{:S(2)}) %collective-permute-start.3) | collective-permute-done | bytes 655392 | tf_op jit(solution)/shard_map/ppermute | solution.py:16
  55.1 1.9 %fusion.4 = (f32[512,4]{0,1:T(4,128)S(1)}, f32[4,512,512]{2,1,0:T(8,128)S(1)}) fusion(pred[512,512]{0,1:T(8,128)(4,1)S(1)} %get-tuple-element.26, bf16[512,4,80]{0,2,1:T(8,128)(2,1)S(1)} %squeeze.34, bf16[2,512,4,80]{1,3,2,0:T(8,128)(2,1)} %collective-permute-done.3), kind=kOutput, calls=%fused_computation.14 | convolution fusion | flops 170915840 | bytes 5120000 | tf_op jit(solution)/shard_map/qhd,khd->qhk/dot_general | solution.py:27
  57.0 6.0 %collective-permute-done = bf16[2,512,4,80]{1,3,2,0:T(8,128)(2,1)} collective-permute-done((bf16[2,512,4,80]{1,3,2,0:T(8,128)(2,1)}, bf16[2,512,4,80]{1,3,2,0:T(8,128)(2,1)}, u32[]{:S(2)}, u32[]{:S(2)}) %collective-permute-start) | collective-permute-done | bytes 655392 | tf_op jit(solution)/shard_map/ppermute | solution.py:16
  63.1 1.9 %fusion.1 = (f32[512,4]{0,1:T(4,128)S(1)}, f32[4,512,512]{2,1,0:T(8,128)S(1)}) fusion(pred[512,512]{0,1:T(8,128)(4,1)S(1)} %get-tuple-element.27, bf16[512,4,80]{0,2,1:T(8,128)(2,1)S(1)} %squeeze.34, bf16[2,512,4,80]{1,3,2,0:T(8,128)(2,1)} %collective-permute-done), kind=kOutput, calls=%fused_computation.11 | convolution fusion | flops 170915840 | bytes 5120000 | tf_op jit(solution)/shard_map/qhd,khd->qhk/dot_general | solution.py:27
  70.3 1.5 %fusion.69 = f32[512,4,80]{0,2,1:T(8,128)S(1)} fusion(bf16[512,4,80]{0,2,1:T(8,128)(2,1)S(1)} %squeeze.35, f32[4,512,512]{2,1,0:T(8,128)S(1)} %get-tuple-element.42, f32[512,4]{0,1:T(4,128)S(1)} %get-tuple-element.22, pred[512,512]{0,1:T(8,128)(4,1)S(1)} %get-tuple-element.23, f32[512,4]{0,1:T(4,128)S(1)} %get-tuple-element.9, ...), kind=kOutput, calls=%fused_computation.48 | convolution fusion | flops 173342720 | bytes 5464064 | tf_op jit(solution)/shard_map/qhk,khd->qhd/dot_general | solution.py:35
  71.9 2.3 %fusion.42 = f32[512,4,80]{0,2,1:T(8,128)S(1)} fusion(f32[4,512,512]{2,1,0:T(8,128)S(1)} %get-tuple-element.34, f32[512,4]{0,1:T(4,128)S(1)} %get-tuple-element.10, pred[512,512]{0,1:T(8,128)(4,1)S(1)} %get-tuple-element.26, bf16[2,512,4,80]{1,3,2,0:T(8,128)(2,1)} %collective-permute-done.3), kind=kOutput, calls=%fused_computation.39 | convolution fusion | flops 173015040 | bytes 5447680 | tf_op jit(solution)/shard_map/qhk,khd->qhd/dot_general | solution.py:35
  74.2 2.3 %fusion.39 = f32[512,4,80]{0,2,1:T(8,128)S(1)} fusion(f32[4,512,512]{2,1,0:T(8,128)S(1)} %get-tuple-element.36, f32[512,4]{0,1:T(4,128)S(1)} %get-tuple-element.11, pred[512,512]{0,1:T(8,128)(4,1)S(1)} %get-tuple-element.25, bf16[2,512,4,80]{1,3,2,0:T(8,128)(2,1)} %collective-permute-done.2), kind=kOutput, calls=%fused_computation.38 | convolution fusion | flops 173015040 | bytes 5447680 | tf_op jit(solution)/shard_map/qhk,khd->qhd/dot_general | solution.py:35
  76.5 2.3 %fusion.36 = f32[512,4,80]{0,2,1:T(8,128)S(1)} fusion(f32[4,512,512]{2,1,0:T(8,128)S(1)} %get-tuple-element.38, f32[512,4]{0,1:T(4,128)S(1)} %get-tuple-element.12, pred[512,512]{0,1:T(8,128)(4,1)S(1)} %get-tuple-element.24, bf16[2,512,4,80]{1,3,2,0:T(8,128)(2,1)} %collective-permute-done.1), kind=kOutput, calls=%fused_computation.37 | convolution fusion | flops 173015040 | bytes 5447680 | tf_op jit(solution)/shard_map/qhk,khd->qhd/dot_general | solution.py:35
  78.8 2.4 %fusion.75 = bf16[512,4,80]{0,2,1:T(8,128)(2,1)S(1)} fusion(f32[512,4,80]{0,2,1:T(8,128)S(1)} %fusion.42, f32[512,4,80]{0,2,1:T(8,128)S(1)} %fusion.39, f32[512,4,80]{0,2,1:T(8,128)S(1)} %fusion.36, f32[512,4,80]{0,2,1:T(8,128)S(1)} %fusion.69, f32[4,512,512]{2,1,0:T(8,128)S(1)} %get-tuple-element.40, f32[512,4]{0,1:T(4,128)S(1)} %get-tuple-element.13, ...), kind=kOutput, calls=%fused_computation.50 | convolution fusion | flops 174489600 | bytes 7774208 | tf_op jit(solution)/shard_map/qhk,khd->qhd/dot_general | solution.py:35
  81.4 9.1 %all_to_all.24 = bf16[4,128,320]{1,2,0:T(8,128)(2,1)S(1)} all-to-all(bf16[4,128,320]{1,2,0:T(8,128)(2,1)S(1)} %copy.38), channel_id=1, replica_groups=mesh['wide'=8,'grp'=4] {'grp'}, dimensions={0} | all-to-all | bytes 655360 | tf_op jit(solution)/shard_map/all_to_all | solution.py:108
  (30 shorter events, 11.5 us)
Async XLA Ops:
  2.4 6.0 %copy-start = (s32[32]{0:T(128)S(1)}, s32[32]{0:T(128)}, u32[]{:S(2)}) copy-start(s32[32]{0:T(128)} %param.7) | copy-start | bytes 388
  4.8 17.2 %all-to-all-start = ((bf16[4,3,128,320]{2,3,1,0:T(8,128)(2,1)}), bf16[4,3,128,320]{2,3,1,0:T(8,128)(2,1)S(1)}, u32[]{:S(2)}, u32[]{:S(2)}) async-start(bf16[4,3,128,320]{2,3,1,0:T(8,128)(2,1)} %pad_maximum_fusion.1), calls=%async_computation | async-start | bytes 1966080 | tf_op jit(solution)/shard_map/all_to_all | solution.py:50
  23.7 18.7 %collective-permute-start.1 = (bf16[2,512,4,80]{1,3,2,0:T(8,128)(2,1)}, bf16[2,512,4,80]{1,3,2,0:T(8,128)(2,1)}, u32[]{:S(2)}, u32[]{:S(2)}) collective-permute-start(bf16[2,512,4,80]{1,3,2,0:T(8,128)(2,1)} %slice.48), channel_id=1, source_target_pairs={{4,0},{8,4},{12,8},{16,12},{20,16},{24,20},{28,24},{5,1},{9,5},{13... | collective-permute-start | bytes 1966088 | tf_op jit(solution)/shard_map/ppermute | solution.py:16
  27.9 27.2 %collective-permute-start.3 = (bf16[2,512,4,80]{1,3,2,0:T(8,128)(2,1)}, bf16[2,512,4,80]{1,3,2,0:T(8,128)(2,1)}, u32[]{:S(2)}, u32[]{:S(2)}) collective-permute-start(bf16[2,512,4,80]{1,3,2,0:T(8,128)(2,1)} %slice.48), channel_id=1, source_target_pairs={{8,0},{12,4},{16,8},{20,12},{24,16},{28,20},{9,1},{13,5},{17,9},{2... | collective-permute-start | bytes 1966088 | tf_op jit(solution)/shard_map/ppermute | solution.py:16
  31.1 17.8 %collective-permute-start.2 = (bf16[2,512,4,80]{1,3,2,0:T(8,128)(2,1)}, bf16[2,512,4,80]{1,3,2,0:T(8,128)(2,1)}, u32[]{:S(2)}, u32[]{:S(2)}) collective-permute-start(bf16[2,512,4,80]{1,3,2,0:T(8,128)(2,1)} %slice.48), channel_id=1, source_target_pairs={{0,8},{4,12},{8,16},{12,20},{16,24},{20,28},{1,9},{5,13},{9,17},{1... | collective-permute-start | bytes 1966088 | tf_op jit(solution)/shard_map/ppermute | solution.py:16
  32.4 30.7 %collective-permute-start = (bf16[2,512,4,80]{1,3,2,0:T(8,128)(2,1)}, bf16[2,512,4,80]{1,3,2,0:T(8,128)(2,1)}, u32[]{:S(2)}, u32[]{:S(2)}) collective-permute-start(bf16[2,512,4,80]{1,3,2,0:T(8,128)(2,1)} %slice.48), channel_id=1, source_target_pairs={{0,4},{4,8},{8,12},{12,16},{16,20},{20,24},{24,28},{1,5},{5,9},{9,... | collective-permute-start | bytes 1966088 | tf_op jit(solution)/shard_map/ppermute | solution.py:16
